TPU v7x, 32 devices: a whole 2x2x4 slice. The times are simulated.
32 devices in a mesh: dp: 4 (over z), row: 4 (over y, x), col: 2 (over core).
Axes of the slice: x: 2, y: 2, z: 4, core: 2. Of those that a mesh axis runs over, the one named last changes fastest.
Arguments:
- tokens: bfloat16 [16, 2048, 768], P(('dp', 'row'), 'col'), may hold values from -6 to 6
- timesteps: int32 [16], P(('dp', 'row')), may hold values from 0 to 999
- block_ids: int32 [16, 2048], P(('dp', 'row')), may hold values from 0 to 11, never falling along the last dimension, each value on 1 to 256 neighbouring positions
- table: float32 [1000, 768], replicated, may hold values from -3 to 3
- gain_one: float32 [768], replicated, may hold values from 0.5 to 1.5
- bias_one: float32 [768], replicated, may hold values from -1.75 to 1.75
- w_query: float32 [768, 768], P('row', 'col'), may hold values from -0.21875 to 0.21875
- w_key: float32 [768, 768], P('row', 'col'), may hold values from -0.21875 to 0.21875
- w_value: float32 [768, 768], P('row', 'col'), may hold values from -0.21875 to 0.21875
- b_query: float32 [768], P('col'), may hold values from -1.75 to 1.75
- b_value: float32 [768], P('col'), may hold values from -1.75 to 1.75
- w_out: float32 [768, 768], P('col', 'row'), may hold values from -3.5 to 3.5
- b_out: float32 [768], replicated, may hold values from -1.75 to 1.75
- gain_two: float32 [768], replicated, may hold values from 0.5 to 1.5
- bias_two: float32 [768], replicated, may hold values from -1.75 to 1.75
- w_up: float32 [768, 3072], P('row', 'col'), may hold values from -0.21875 to 0.21875
- b_up: float32 [3072], P('col'), may hold values from -1.75 to 1.75
- w_down: float32 [3072, 768], P('col', 'row'), may hold values from -0.109375 to 0.109375
- b_down: float32 [768], replicated, may hold values from -1.75 to 1.75
- cotangent: bfloat16 [16, 2048, 768], P(('dp', 'row'), 'col'), may hold values from -6 to 6
Outputs:
- layer_out: bfloat16 [16, 2048, 768], P(('dp', 'row'), 'col')
- grad_tokens: float32 [16, 2048, 768], P(('dp', 'row'), 'col')
- grad_table: float32 [1000, 768], replicated
- grad_gain_one: float32 [768], replicated
- grad_bias_one: float32 [768], replicated
- grad_w_query: float32 [768, 768], P('row', 'col')
- grad_w_key: float32 [768, 768], P('row', 'col')
- grad_w_value: float32 [768, 768], P('row', 'col')
- grad_b_query: float32 [768], P('col')
- grad_b_value: float32 [768], P('col')
- grad_w_out: float32 [768, 768], P('col', 'row')
- grad_b_out: float32 [768], replicated
- grad_gain_two: float32 [768], replicated
- grad_bias_two: float32 [768], replicated
- grad_w_up: float32 [768, 3072], P('row', 'col')
- grad_b_up: float32 [3072], P('col')
- grad_w_down: float32 [3072, 768], P('col', 'row')
- grad_b_down: float32 [768], replicated
Inputs may be any that keep to these rules, and one draw needn't show every extreme that they name: `block_ids`: block numbers never fall along a sequence; every block number of a sequence is used, each block holds 1 to 256 positions, and some block holds exactly 256.
All inputs are finite; a program needn't handle non-finite values.
Results may differ from a plain program's by a relative error of at most 0.012.
The roundings to bfloat16 on the way count: a program that leaves them out, or rounds other values in their place, can miss the bound.
Values may be sent and summed in bfloat16 or wider, within the bound.
No kernel may reach another device: no remote copies, remote signals or barrier semaphores. Data moves between devices by JAX's collectives and lax.ppermute only.
A program may use at most 256 MiB of HBM per device.

v0:
```python
import jax
import jax.numpy as jnp
from jax import lax
from jax.sharding import PartitionSpec as P

HEAD_DIM = 64
norm_eps = 1e-05
masked_score = -1000000000.0


def layer_norm_parts(values, gain, bias):
    mean = jnp.mean(values, axis=-1, keepdims=True)
    centred = values - mean
    inverse = lax.rsqrt(jnp.mean(centred * centred, axis=-1, keepdims=True) + norm_eps)
    unit = centred * inverse
    return (unit * gain + bias, unit, inverse)


def norm_back(grad_normed, unit, inverse, gain):
    grad_unit = grad_normed * gain
    first_mean = jnp.mean(grad_unit, axis=-1, keepdims=True)
    second_mean = jnp.mean(grad_unit * unit, axis=-1, keepdims=True)
    return inverse * (grad_unit - first_mean - unit * second_mean)


def gelu_exact(values):
    return jax.nn.gelu(values, approximate=False)


def shards(
    tokens,
    timesteps,
    block_ids,
    table,
    gain_one,
    bias_one,
    w_query,
    w_key,
    w_value,
    b_query,
    b_value,
    w_out,
    b_out,
    gain_two,
    bias_two,
    w_up,
    b_up,
    w_down,
    b_down,
    cotangent,
):
    seq_count, local_len, model_width = tokens.shape
    full_len = block_ids.shape[1]
    head_cols = w_query.shape[1]
    hidden_cols = w_up.shape[1]
    local_heads = head_cols // HEAD_DIM
    row_block = min(512, full_len)
    block_count = full_len // row_block
    scale_factor = HEAD_DIM ** (-0.5)
    col_index = lax.axis_index("col")
    row_index = lax.axis_index("row")
    row_size = lax.axis_size("row")
    query_low = w_query.astype(jnp.bfloat16)
    key_low = w_key.astype(jnp.bfloat16)
    value_low = w_value.astype(jnp.bfloat16)
    up_low = w_up.astype(jnp.bfloat16)
    out_low = w_out.astype(jnp.bfloat16)
    down_low = w_down.astype(jnp.bfloat16)
    query_full, key_full, value_full, up_full, out_full, down_full = (
        lax.all_gather(query_low, "row", axis=0, tiled=True),
        lax.all_gather(key_low, "row", axis=0, tiled=True),
        lax.all_gather(value_low, "row", axis=0, tiled=True),
        lax.all_gather(up_low, "row", axis=0, tiled=True),
        lax.all_gather(out_low, "row", axis=1, tiled=True),
        lax.all_gather(down_low, "row", axis=1, tiled=True),
    )
    step_onehot = (
        lax.broadcasted_iota(jnp.int32, (seq_count, table.shape[0]), 1) == timesteps[:, None]
    ).astype(jnp.float32)
    table_rows = jnp.dot(
        step_onehot, table, precision=lax.Precision.HIGHEST, preferred_element_type=jnp.float32
    )
    start = tokens.astype(jnp.float32) + table_rows[:, None, :]
    normed_one, unit_one, inverse_one = layer_norm_parts(start, gain_one, bias_one)
    rows_one = lax.all_gather(normed_one.astype(jnp.bfloat16), "col", axis=1, tiled=True).reshape(
        seq_count * full_len, model_width
    )
    query = (jnp.dot(rows_one, query_full, preferred_element_type=jnp.float32) + b_query).astype(
        jnp.bfloat16
    )
    key = jnp.dot(rows_one, key_full, preferred_element_type=jnp.float32).astype(jnp.bfloat16)
    value = (jnp.dot(rows_one, value_full, preferred_element_type=jnp.float32) + b_value).astype(
        jnp.bfloat16
    )
    query_seq = query.reshape(seq_count, block_count, row_block, local_heads, HEAD_DIM)
    key_seq = key.reshape(seq_count, full_len, local_heads, HEAD_DIM)
    value_seq = value.reshape(seq_count, full_len, local_heads, HEAD_DIM)
    query_ids_all = block_ids.reshape(seq_count, block_count, row_block)

    def scores_for(query_part, key_part, query_ids, key_ids):
        scores = (
            jnp.einsum("qhd,khd->hqk", query_part, key_part, preferred_element_type=jnp.float32)
            * scale_factor
        )
        allowed = key_ids[None, None, :] <= query_ids[None, :, None]
        return jnp.where(allowed, scores, masked_score)

    def forward_seq(pieces):
        query_blocks, key_part, value_part, ids_blocks, key_ids = pieces

        def forward_block(inner):
            query_part, query_ids = inner
            scores = scores_for(query_part, key_part, query_ids, key_ids)
            top = jnp.max(scores, axis=-1, keepdims=True)
            expo = jnp.exp(scores - top)
            total = jnp.sum(expo, axis=-1, keepdims=True)
            probs = (expo / total).astype(jnp.bfloat16)
            mixed = jnp.einsum(
                "hqk,khd->qhd", probs, value_part, preferred_element_type=jnp.float32
            )
            return (mixed, (top + jnp.log(total))[..., 0])

        return lax.map(forward_block, (query_blocks, ids_blocks))

    attended, log_sums = lax.map(
        forward_seq, (query_seq, key_seq, value_seq, query_ids_all, block_ids)
    )
    attended_low = attended.reshape(seq_count * full_len, head_cols).astype(jnp.bfloat16)
    branch_part = jnp.dot(attended_low, out_full, preferred_element_type=jnp.float32).reshape(
        seq_count, full_len, model_width
    )
    branch = lax.psum_scatter(branch_part, "col", scatter_dimension=1, tiled=True)
    middle = start + branch + b_out
    normed_two, unit_two, inverse_two = layer_norm_parts(middle, gain_two, bias_two)
    rows_two = lax.all_gather(normed_two.astype(jnp.bfloat16), "col", axis=1, tiled=True).reshape(
        seq_count * full_len, model_width
    )
    hidden_pre = jnp.dot(rows_two, up_full, preferred_element_type=jnp.float32) + b_up
    hidden_low = gelu_exact(hidden_pre).astype(jnp.bfloat16)
    mixer_part = jnp.dot(hidden_low, down_full, preferred_element_type=jnp.float32).reshape(
        seq_count, full_len, model_width
    )
    mixer = lax.psum_scatter(
        mixer_part.astype(jnp.bfloat16), "col", scatter_dimension=1, tiled=True
    ).astype(jnp.float32)
    layer_out = (middle + mixer + b_down).astype(jnp.bfloat16)
    grad_out = cotangent.astype(jnp.float32)
    grad_mixer_rows = lax.all_gather(cotangent, "col", axis=1, tiled=True).reshape(
        seq_count * full_len, model_width
    )
    grad_b_down = jnp.sum(cotangent, axis=(0, 1), dtype=jnp.float32)
    grad_down = jnp.einsum(
        "rf,rd->fd", hidden_low, grad_mixer_rows, preferred_element_type=jnp.float32
    )
    grad_hidden = jnp.einsum(
        "rd,fd->rf", grad_mixer_rows, down_full, preferred_element_type=jnp.float32
    )
    grad_pre = jax.vjp(gelu_exact, hidden_pre)[1](grad_hidden)[0]
    grad_pre_low = grad_pre.astype(jnp.bfloat16)
    grad_up = jnp.einsum("rd,rf->df", rows_two, grad_pre_low, preferred_element_type=jnp.float32)
    grad_b_up_local = jnp.sum(grad_pre_low, axis=0, dtype=jnp.float32)
    grad_normed_two_part = jnp.einsum(
        "rf,df->rd", grad_pre_low, up_full, preferred_element_type=jnp.float32
    ).reshape(seq_count, full_len, model_width)
    grad_normed_two = lax.psum_scatter(grad_normed_two_part, "col", scatter_dimension=1, tiled=True)
    grad_gain_two = jnp.sum(grad_normed_two * unit_two, axis=(0, 1))
    grad_bias_two = jnp.sum(grad_normed_two, axis=(0, 1))
    grad_middle = grad_out + norm_back(grad_normed_two, unit_two, inverse_two, gain_two)
    grad_branch_low = grad_middle.astype(jnp.bfloat16)
    grad_b_out = jnp.sum(grad_branch_low, axis=(0, 1), dtype=jnp.float32)
    grad_branch_rows = lax.all_gather(grad_branch_low, "col", axis=1, tiled=True).reshape(
        seq_count * full_len, model_width
    )
    grad_out_proj = jnp.einsum(
        "rh,rd->hd", attended_low, grad_branch_rows, preferred_element_type=jnp.float32
    )
    grad_attended = jnp.einsum(
        "rd,hd->rh", grad_branch_rows, out_full, preferred_element_type=jnp.float32
    ).astype(jnp.bfloat16)
    grad_att_seq = grad_attended.reshape(seq_count, block_count, row_block, local_heads, HEAD_DIM)

    def backward_seq(pieces):
        query_blocks, key_part, value_part, ids_blocks, key_ids, grad_blocks, sums_blocks = pieces

        def backward_block(carry, inner):
            query_part, query_ids, grad_part, log_part = inner
            scores = scores_for(query_part, key_part, query_ids, key_ids)
            probs = jnp.exp(scores - log_part[:, :, None])
            grad_probs = jnp.einsum(
                "qhd,khd->hqk", grad_part, value_part, preferred_element_type=jnp.float32
            )
            inner_sum = jnp.sum(probs * grad_probs, axis=-1, keepdims=True)
            grad_scores = (probs * (grad_probs - inner_sum)).astype(jnp.bfloat16)
            grad_query_part = (
                jnp.einsum(
                    "hqk,khd->qhd", grad_scores, key_part, preferred_element_type=jnp.float32
                )
                * scale_factor
            )
            key_acc = (
                carry[0]
                + jnp.einsum(
                    "hqk,qhd->khd", grad_scores, query_part, preferred_element_type=jnp.float32
                )
                * scale_factor
            )
            value_acc = carry[1] + jnp.einsum(
                "hqk,qhd->khd",
                probs.astype(jnp.bfloat16),
                grad_part,
                preferred_element_type=jnp.float32,
            )
            return ((key_acc, value_acc), grad_query_part)

        empty = jnp.zeros((full_len, local_heads, HEAD_DIM), jnp.float32)
        (grad_key_part, grad_value_part), grad_query_blocks = lax.scan(
            backward_block, (empty, empty), (query_blocks, ids_blocks, grad_blocks, sums_blocks)
        )
        return (grad_query_blocks, grad_key_part, grad_value_part)

    grad_query_all, grad_key_all, grad_value_all = lax.map(
        backward_seq,
        (query_seq, key_seq, value_seq, query_ids_all, block_ids, grad_att_seq, log_sums),
    )
    grad_query_low = grad_query_all.reshape(seq_count * full_len, head_cols).astype(jnp.bfloat16)
    grad_key_low = grad_key_all.reshape(seq_count * full_len, head_cols).astype(jnp.bfloat16)
    grad_value_low = grad_value_all.reshape(seq_count * full_len, head_cols).astype(jnp.bfloat16)
    grad_w_query = jnp.einsum(
        "rd,rh->dh", rows_one, grad_query_low, preferred_element_type=jnp.float32
    )
    grad_w_key = jnp.einsum("rd,rh->dh", rows_one, grad_key_low, preferred_element_type=jnp.float32)
    grad_w_value = jnp.einsum(
        "rd,rh->dh", rows_one, grad_value_low, preferred_element_type=jnp.float32
    )
    grad_b_query_local = jnp.sum(grad_query_low, axis=0, dtype=jnp.float32)
    grad_b_value_local = jnp.sum(grad_value_low, axis=0, dtype=jnp.float32)
    grad_normed_one_part = (
        jnp.einsum("rh,dh->rd", grad_query_low, query_full, preferred_element_type=jnp.float32)
        + jnp.einsum("rh,dh->rd", grad_key_low, key_full, preferred_element_type=jnp.float32)
        + jnp.einsum("rh,dh->rd", grad_value_low, value_full, preferred_element_type=jnp.float32)
    ).reshape(seq_count, full_len, model_width)
    grad_normed_one = lax.psum_scatter(grad_normed_one_part, "col", scatter_dimension=1, tiled=True)
    grad_gain_one = jnp.sum(grad_normed_one * unit_one, axis=(0, 1))
    grad_bias_one = jnp.sum(grad_normed_one, axis=(0, 1))
    grad_tokens = grad_middle + norm_back(grad_normed_one, unit_one, inverse_one, gain_one)
    token_sums = jnp.sum(grad_tokens, axis=1)

    def widen(local_vec, full_size):
        return lax.dynamic_update_slice_in_dim(
            jnp.zeros((full_size,), jnp.float32), local_vec, col_index * local_vec.shape[0], 0
        )

    wide_query_bias = widen(grad_b_query_local, model_width)
    wide_value_bias = widen(grad_b_value_local, model_width)
    wide_up_bias = widen(grad_b_up_local, hidden_cols * lax.axis_size("col"))
    grad_table = jnp.einsum(
        "sv,sd->vd",
        step_onehot,
        token_sums,
        precision=lax.Precision.HIGHEST,
        preferred_element_type=jnp.float32,
    )
    (
        sum_table,
        sum_gain_one,
        sum_bias_one,
        sum_query_bias,
        sum_value_bias,
        sum_out_bias,
        sum_gain_two,
        sum_bias_two,
        sum_up_bias,
        sum_down_bias,
    ) = lax.psum(
        (
            grad_table,
            grad_gain_one,
            grad_bias_one,
            wide_query_bias,
            wide_value_bias,
            grad_b_out,
            grad_gain_two,
            grad_bias_two,
            wide_up_bias,
            grad_b_down,
        ),
        ("dp", "row", "col"),
    )
    grad_b_query = lax.dynamic_slice_in_dim(sum_query_bias, col_index * head_cols, head_cols, 0)
    grad_b_value = lax.dynamic_slice_in_dim(sum_value_bias, col_index * head_cols, head_cols, 0)
    grad_b_up = lax.dynamic_slice_in_dim(sum_up_bias, col_index * hidden_cols, hidden_cols, 0)

    def owned_rows(grad_whole, dim_pick):
        share = grad_whole.shape[dim_pick] // row_size
        return lax.dynamic_slice_in_dim(grad_whole, row_index * share, share, dim_pick)

    summed = lax.psum(
        (grad_w_query, grad_w_key, grad_w_value, grad_up, grad_out_proj, grad_down), ("dp", "row")
    )
    owned_query = owned_rows(summed[0], 0)
    owned_key = owned_rows(summed[1], 0)
    owned_value = owned_rows(summed[2], 0)
    owned_up = owned_rows(summed[3], 0)
    owned_out = owned_rows(summed[4], 1)
    owned_down = owned_rows(summed[5], 1)
    return (
        layer_out,
        grad_tokens,
        sum_table,
        sum_gain_one,
        sum_bias_one,
        owned_query,
        owned_key,
        owned_value,
        grad_b_query,
        grad_b_value,
        owned_out,
        sum_out_bias,
        sum_gain_two,
        sum_bias_two,
        owned_up,
        grad_b_up,
        owned_down,
        sum_down_bias,
    )


def solution(mesh):
    return jax.shard_map(
        shards,
        mesh=mesh,
        in_specs=(
            P(("dp", "row"), "col", None),
            P(("dp", "row")),
            P(("dp", "row"), None),
            P(),
            P(),
            P(),
            P("row", "col"),
            P("row", "col"),
            P("row", "col"),
            P("col"),
            P("col"),
            P("col", "row"),
            P(),
            P(),
            P(),
            P("row", "col"),
            P("col"),
            P("col", "row"),
            P(),
            P(("dp", "row"), "col", None),
        ),
        out_specs=(
            P(("dp", "row"), "col", None),
            P(("dp", "row"), "col", None),
            P(),
            P(),
            P(),
            P("row", "col"),
            P("row", "col"),
            P("row", "col"),
            P("col"),
            P("col"),
            P("col", "row"),
            P(),
            P(),
            P(),
            P("row", "col"),
            P("col"),
            P("col", "row"),
            P(),
        ),
        check_vma=False,
    )
```

profile of v0, /device:TPU:0, one launch (start us, length us, event | category | flops | bytes accessed | tf_op | source)
XLA Modules:
  0.0 1383.5 jit_solution(9425003297407014153)
XLA Ops:
  16.0 12.7 all_gather.34
  28.7 11.2 all_gather.33
  39.9 10.9 all_gather.32
  50.8 10.1 all_gather.31
  61.7 4.8 add_convert_fusion.4
  81.4 149.2 %while.47 = (s32[]{:T(128)}, bf16[4,512,6,64]{1,3,2,0:T(8,128)(2,1)}, f32[4,6,512]{2,1,0:T(8,128)}, s32[2048]{0:T(1024)S(1)}, s32[4,512]{1,0:T(4,128)S(1)}, /*in...) while((s32[]{:T(128)}, ...), condition=%wide.region_5.6_spmd, body=%wide.region_2.5_spmd.sunk | while | flops 1687155712 | bytes 103016640 | solution.py:123
  82.0 11.6 fusion.135
  93.7 12.1 fusion.136
  105.8 11.6 fusion.137
  119.2 11.6 fusion.135
  130.9 12.1 fusion.136
  143.0 11.6 fusion.137
  156.4 11.6 fusion.135
  168.1 12.1 fusion.136
  180.2 11.6 fusion.137
  193.6 11.6 fusion.135
  205.3 12.1 fusion.136
  217.4 11.6 fusion.137
  235.5 4.5 convolution_bitcast_fusion.1
  242.2 12.7 reduce-scatter.5.cloned.1.call-done
  262.4 18.1 %all-gather.11.cloned.1.call-done = bf16[768,1536]{1,0:T(8,128)(2,1)} async-done(((bf16[192,1536]{1,0:T(8,128)(2,1)}), bf16[768,1536]{1,0:T(8,128)(2,1)}) %all-gather.11.cloned.1.call-update) | async-done | bytes 2359312 | tf_op jit(solution)/shard_map/all_gather | solution.py:73
  280.5 14.1 %all-gather.9.cloned.1.call-done = bf16[1,2048,768]{2,1,0:T(8,128)(2,1)} async-done(((bf16[1,1024,768]{2,1,0:T(8,128)(2,1)}), bf16[1,2048,768]{2,1,0:T(8,128)(2,1)}) %all-gather.9.cloned.1.call-update) | async-done | bytes 3145744 | tf_op jit(solution)/shard_map/all_gather | solution.py:135
  294.6 34.8 %multiply_convert_fusion.1 = (bf16[2048,1536]{1,0:T(8,128)(2,1)}, f32[2048,1536]{1,0:T(8,128)}, f32[2048,1536]{1,0:T(8,128)}) fusion(f32[1536]{0:T(1024)S(1)} %copy-done.70, bf16[768,1536]{1,0:T(8,128)(2,1)} %all-gather.11.cloned.1.call-done, bf16[1,2048,768]{2,1,0:T(8,128)(2,1)} %all-gather.9.cloned.1.call-done), kind=kOutput, calls=%fused_computation.51 | convolution fusion | flops 5039456256 | bytes 36968448 | tf_op jit(solution)/shard_map/dot_general | solution.py:138
  329.4 21.0 %all-gather.13.cloned.1.call-done = bf16[1536,768]{0,1:T(8,128)(2,1)} async-done(((bf16[1536,192]{0,1:T(8,128)(2,1)}), bf16[1536,768]{0,1:T(8,128)(2,1)}) %all-gather.13.cloned.1.call-update) | async-done | bytes 2359312 | tf_op jit(solution)/shard_map/all_gather | solution.py:75
  350.4 17.7 %convert_reduce_fusion = (f32[1536]{0:T(1024)}, bf16[2048,1536]{1,0:T(8,128)(2,1)S(1)}) fusion(f32[2048,1536]{1,0:T(8,128)} %get-tuple-element.325, bf16[1536,768]{0,1:T(8,128)(2,1)} %all-gather.13.cloned.1.call-done, bf16[1,2048,768]{2,1,0:T(8,128)(2,1)} %all-gather.15.cloned.1.call-done, f32[2048,1536]{1,0:T(8,128)} %get-tuple-element.334, ...), kind=kOutput, calls=%fused_computation.49 | convolution fusion | flops 4885314048 | bytes 36974592 | tf_op jit(solution)/shard_map/rd,fd->rf/dot_general | solution.py:155
  370.7 7.0 convolution_bitcast_fusion
  379.4 9.4 fusion.67
  392.2 4.2 multiply_reduce_fusion.1
  396.4 10.1 reduce-scatter.7.cloned.1.call-done
  406.5 6.4 convert_reduce_fusion.2
  413.0 13.5 all-gather.17.cloned.1.call-done
  426.5 4.9 fusion.75
  439.8 339.8 %while.48 = (s32[]{:T(128)}, f32[2048,6,64]{0,2,1:T(8,128)}, f32[2048,6,64]{0,2,1:T(8,128)}, bf16[4,512,6,64]{1,3,2,0:T(8,128)(2,1)}, bf16[4,512,6,64]{1,3,2,0:T...) while((s32[]{:T(128)}, f32[2048,6,64]{0,2,1:T(8,128)}, ...), condition=%wide.region_15.16_spmd.clone, body=%wide.region_13.15_spmd.clone.sunk | while | flops 4126077952 | bytes 212699312 | solution.py:216
  442.3 11.2 fusion.147
  453.5 12.9 bitcast_add_fusion.5
  466.4 18.1 %multiply_reduce_fusion.10 = (f32[6,512]{1,0:T(8,128)S(1)}, f32[6,512,2048]{2,1,0:T(8,128)}) fusion(f32[6,512,2048]{2,1,0:T(8,128)} %fusion.147, f32[6,512]{1,0:T(8,128)S(1)} %dynamic-slice_bitcast_fusion.2, pred[512,2048]{1,0:T(8,128)(4,1)S(1)} %broadcast_compare_fusion.5, bf16[2048,6,64]{0,2,1:T(8,128)(2,1)} %get-tuple-element.526, ...), kind=kOutput, calls=%fused_computation.18.clone.1 | convolution fusion | flops 836760576 | bytes 53370884 | tf_op jit(solution)/shard_map/while/body/eval_jaxpr/while/body/eval_jaxpr/qhd,khd->hqk/dot_general | solution.py:189
  484.5 21.3 %multiply_convert_fusion.3 = bf16[6,512,2048]{2,1,0:T(8,128)(2,1)} fusion(f32[6,512,2048]{2,1,0:T(8,128)} %get-tuple-element.461, f32[6,512,2048]{2,1,0:T(8,128)} %fusion.147, f32[6,512]{1,0:T(8,128)S(1)} %get-tuple-element.462, f32[6,512]{1,0:T(8,128)S(1)} %dynamic-slice_bitcast_fusion.2, pred[512,2048]{1,0:T(8,128)(4,1)S(1)} %broadcast_compare_fusion.5), kind=kLoop, calls=%fused_computation.17.clone.1 | loop fusion | flops 37748736 | bytes 63987712 | tf_op jit(solution)/shard_map/while/body/eval_jaxpr/while/body/eval_jaxpr/convert_element_type | solution.py:193
  505.7 9.2 fusion.148
  515.0 8.7 bitcast_add_fusion.4
  525.7 11.2 fusion.147
  536.9 13.8 bitcast_add_fusion.5
  550.7 18.1 %multiply_reduce_fusion.10 = (f32[6,512]{1,0:T(8,128)S(1)}, f32[6,512,2048]{2,1,0:T(8,128)}) fusion(f32[6,512,2048]{2,1,0:T(8,128)} %fusion.147, f32[6,512]{1,0:T(8,128)S(1)} %dynamic-slice_bitcast_fusion.2, pred[512,2048]{1,0:T(8,128)(4,1)S(1)} %broadcast_compare_fusion.5, bf16[2048,6,64]{0,2,1:T(8,128)(2,1)} %get-tuple-element.526, ...), kind=kOutput, calls=%fused_computation.18.clone.1 | convolution fusion | flops 836760576 | bytes 53370884 | tf_op jit(solution)/shard_map/while/body/eval_jaxpr/while/body/eval_jaxpr/qhd,khd->hqk/dot_general | solution.py:189
  568.8 21.3 %multiply_convert_fusion.3 = bf16[6,512,2048]{2,1,0:T(8,128)(2,1)} fusion(f32[6,512,2048]{2,1,0:T(8,128)} %get-tuple-element.461, f32[6,512,2048]{2,1,0:T(8,128)} %fusion.147, f32[6,512]{1,0:T(8,128)S(1)} %get-tuple-element.462, f32[6,512]{1,0:T(8,128)S(1)} %dynamic-slice_bitcast_fusion.2, pred[512,2048]{1,0:T(8,128)(4,1)S(1)} %broadcast_compare_fusion.5), kind=kLoop, calls=%fused_computation.17.clone.1 | loop fusion | flops 37748736 | bytes 63987712 | tf_op jit(solution)/shard_map/while/body/eval_jaxpr/while/body/eval_jaxpr/convert_element_type | solution.py:193
  590.1 9.2 fusion.148
  599.3 9.6 bitcast_add_fusion.4
  611.0 11.2 fusion.147
  622.2 13.8 bitcast_add_fusion.5
  636.0 18.1 %multiply_reduce_fusion.10 = (f32[6,512]{1,0:T(8,128)S(1)}, f32[6,512,2048]{2,1,0:T(8,128)}) fusion(f32[6,512,2048]{2,1,0:T(8,128)} %fusion.147, f32[6,512]{1,0:T(8,128)S(1)} %dynamic-slice_bitcast_fusion.2, pred[512,2048]{1,0:T(8,128)(4,1)S(1)} %broadcast_compare_fusion.5, bf16[2048,6,64]{0,2,1:T(8,128)(2,1)} %get-tuple-element.526, ...), kind=kOutput, calls=%fused_computation.18.clone.1 | convolution fusion | flops 836760576 | bytes 53370884 | tf_op jit(solution)/shard_map/while/body/eval_jaxpr/while/body/eval_jaxpr/qhd,khd->hqk/dot_general | solution.py:189
  654.1 21.3 %multiply_convert_fusion.3 = bf16[6,512,2048]{2,1,0:T(8,128)(2,1)} fusion(f32[6,512,2048]{2,1,0:T(8,128)} %get-tuple-element.461, f32[6,512,2048]{2,1,0:T(8,128)} %fusion.147, f32[6,512]{1,0:T(8,128)S(1)} %get-tuple-element.462, f32[6,512]{1,0:T(8,128)S(1)} %dynamic-slice_bitcast_fusion.2, pred[512,2048]{1,0:T(8,128)(4,1)S(1)} %broadcast_compare_fusion.5), kind=kLoop, calls=%fused_computation.17.clone.1 | loop fusion | flops 37748736 | bytes 63987712 | tf_op jit(solution)/shard_map/while/body/eval_jaxpr/while/body/eval_jaxpr/convert_element_type | solution.py:193
  675.4 9.3 fusion.148
  684.6 9.6 bitcast_add_fusion.4
  696.3 11.2 fusion.147
  707.5 13.8 bitcast_add_fusion.5
  721.3 18.1 %multiply_reduce_fusion.10 = (f32[6,512]{1,0:T(8,128)S(1)}, f32[6,512,2048]{2,1,0:T(8,128)}) fusion(f32[6,512,2048]{2,1,0:T(8,128)} %fusion.147, f32[6,512]{1,0:T(8,128)S(1)} %dynamic-slice_bitcast_fusion.2, pred[512,2048]{1,0:T(8,128)(4,1)S(1)} %broadcast_compare_fusion.5, bf16[2048,6,64]{0,2,1:T(8,128)(2,1)} %get-tuple-element.526, ...), kind=kOutput, calls=%fused_computation.18.clone.1 | convolution fusion | flops 836760576 | bytes 53370884 | tf_op jit(solution)/shard_map/while/body/eval_jaxpr/while/body/eval_jaxpr/qhd,khd->hqk/dot_general | solution.py:189
  739.4 21.3 %multiply_convert_fusion.3 = bf16[6,512,2048]{2,1,0:T(8,128)(2,1)} fusion(f32[6,512,2048]{2,1,0:T(8,128)} %get-tuple-element.461, f32[6,512,2048]{2,1,0:T(8,128)} %fusion.147, f32[6,512]{1,0:T(8,128)S(1)} %get-tuple-element.462, f32[6,512]{1,0:T(8,128)S(1)} %dynamic-slice_bitcast_fusion.2, pred[512,2048]{1,0:T(8,128)(4,1)S(1)} %broadcast_compare_fusion.5), kind=kLoop, calls=%fused_computation.17.clone.1 | loop fusion | flops 37748736 | bytes 63987712 | tf_op jit(solution)/shard_map/while/body/eval_jaxpr/while/body/eval_jaxpr/convert_element_type | solution.py:193
  760.7 9.3 fusion.148
  769.9 9.6 bitcast_add_fusion.4
  790.2 4.5 add_bitcast_fusion
  794.7 9.8 fusion.48
  804.6 11.0 fusion.45
  832.1 3.9 fusion.79
  839.1 46.3 %all-reduce = (f32[768]{0:T(1024)}, f32[768]{0:T(1024)}, f32[768]{0:T(1024)S(1)}, f32[768]{0:T(1024)S(1)}, f32[768]{0:T(1024)}, /*index=5*/f32[768]{0:T(1024)}, f32[768]{0:T(1024)}, f32[3072]{0:T(1024)S(1)}, f32[768]{0:T(1024)}) all-reduce(f32[768]{0:T(1024)S(1)} %get-tuple-element.258, ...), channel_id=1, replica_groups=mesh['dp'=4,'row'=4,'col'=2] {'dp','row','col'}, use_global_device_ids=true, to_apply=%region_22.23 | all-reduce | flops 9216 | bytes 73728 | tf_op jit(solution)/shard_map/psum | solution.py:274
  887.4 341.9 %all-reduce.7.cloned.1.call-done = (f32[768,384]{1,0:T(8,128)}, f32[768,384]{1,0:T(8,128)}, f32[768,384]{1,0:T(8,128)}, f32[384,768]{0,1:T(8,128)}, f32[768,1536]{1,0:T(8,128)}, /*index=5*/f32[1536,768]{0,1:T(8,128)}) async-done(((f32[768,384]{1,0:T(8,128)}, f32[768,384]{1,0:T(8,128)}, f32[768,384]{1,0:T(8,128)}, f32[384,768]{0,1:T(8,128)}, f32[768,1536]{1,0:T(8,128)}, /*index=5*/f32[1536,768]{0,1:T(8,128)}), ...) | async-done | bytes 14155792 | tf_op jit(solution)/shard_map/psum | solution.py:297
  1240.9 131.2 %all-reduce.5.cloned.1.call-done = f32[1000,768]{1,0:T(8,128)} async-done(((f32[1000,768]{1,0:T(8,128)}), f32[1000,768]{1,0:T(8,128)}) %all-reduce.5.cloned.1.call-update) | async-done | bytes 3072016 | tf_op jit(solution)/shard_map/psum | solution.py:274
  (290 shorter events, 115.9 us)
Async XLA Ops:
  8.0 4.7 copy-start.51
  8.1 4.7 copy-start.60
  8.1 52.9 %all-gather.7.cloned.1.call-start = ((), (), s32[]{:S(2)}) async-start(), calls=%async_computation.4 | async-start | bytes 4718592 | tf_op jit(solution)/shard_map/all_gather | solution.py:85
  8.1 3.4 copy-start.5
  12.0 3.2 copy-start.33
  12.0 3.9 copy-start.35
  12.0 4.0 copy-start.36
  12.7 3.3 copy-start.37
  12.7 3.3 copy-start.38
  12.7 3.1 copy-start.47
  14.6 47.2 %copy-start.71 = (f32[384]{0:T(512)S(1)}, f32[384]{0:T(512)}, u32[]{:S(2)}) copy-start(f32[384]{0:T(512)} %param.33) | copy-start | bytes 4612
  14.6 240.3 %reduce-scatter.5.cloned.1.call-start = ((), (), s32[]{:S(2)}) async-start(), calls=%async_computation.5 | async-start | bytes 9437184 | tf_op jit(solution)/shard_map/reduce_scatter | solution.py:132
  70.8 3.0 copy-start.25
  73.8 3.5 copy-start.23
  73.8 3.5 copy-start.64
  73.8 3.5 copy-start.72
  93.7 12.1 copy-start.8
  93.7 12.1 copy-start.20
  130.9 12.1 copy-start.8
  130.9 12.1 copy-start.20
  168.1 12.1 copy-start.8
  168.1 12.1 copy-start.20
  205.3 12.1 copy-start.8
  205.3 12.1 copy-start.20
  230.6 3.7 copy-start.2
  230.6 3.7 copy-start.46
  230.6 4.9 copy-start.29
  239.9 14.9 %copy-start.6 = (bf16[1,1024,768]{2,1,0:T(8,128)(2,1)S(1)}, bf16[1,1024,768]{2,1,0:T(8,128)(2,1)}, u32[]{:S(2)}) copy-start(bf16[1,1024,768]{2,1,0:T(8,128)(2,1)} %param.24) | copy-start | bytes 4718596
  239.9 14.9 %copy-start.40 = (f32[768]{0:T(1024)S(1)}, f32[768]{0:T(1024)}, u32[]{:S(2)}) copy-start(f32[768]{0:T(1024)} %copy-done.39) | copy-start | bytes 9220
  239.9 14.9 %copy-start.61 = (f32[768]{0:T(1024)S(1)}, f32[768]{0:T(1024)}, u32[]{:S(2)}) copy-start(f32[768]{0:T(1024)} %param.36) | copy-start | bytes 9220
  240.0 40.5 %all-gather.11.cloned.1.call-start = ((), (), s32[]{:S(2)}) async-start(), calls=%async_computation.7 | async-start | bytes 2949120 | tf_op jit(solution)/shard_map/all_gather | solution.py:73
  242.1 52.5 %all-gather.9.cloned.1.call-start = ((), (), s32[]{:S(2)}) async-start(), calls=%async_computation.6 | async-start | bytes 4718592 | tf_op jit(solution)/shard_map/all_gather | solution.py:135
  257.4 3.3 copy-start.44
  260.7 33.8 %copy-start.70 = (f32[1536]{0:T(1024)S(1)}, f32[1536]{0:T(1024)}, u32[]{:S(2)}) copy-start(f32[1536]{0:T(1024)} %param.40) | copy-start | bytes 18436
  260.8 68.6 %all-gather.15.cloned.1.call-start = ((), (), s32[]{:S(2)}) async-start(), calls=%async_computation.10 | async-start | bytes 4718592 | tf_op jit(solution)/shard_map/all_gather | solution.py:148
  261.4 89.0 %all-gather.13.cloned.1.call-start = ((), (), s32[]{:S(2)}) async-start(), calls=%async_computation.8 | async-start | bytes 2949120 | tf_op jit(solution)/shard_map/all_gather | solution.py:75
  262.3 129.9 %reduce-scatter.9.cloned.1.call-start = ((), (), s32[]{:S(2)}) async-start(), calls=%async_computation.11 | async-start | bytes 9437184 | tf_op jit(solution)/shard_map/reduce_scatter | solution.py:165
  350.4 20.3 %copy-start.68 = (bf16[768,1536]{1,0:T(8,128)(2,1)S(1)}, bf16[768,1536]{1,0:T(8,128)(2,1)}, u32[]{:S(2)}) copy-start(bf16[768,1536]{1,0:T(8,128)(2,1)} %all-gather.11.cloned.1.call-done) | copy-start | bytes 7077892
  377.7 28.7 %reduce-scatter.7.cloned.1.call-start = ((), (), s32[]{:S(2)}) async-start(), calls=%async_computation.9 | async-start | bytes 4718592 | tf_op jit(solution)/shard_map/reduce_scatter | solution.py:143
  388.8 3.4 copy-start.45
  388.8 3.4 copy-start.50
  388.8 3.4 copy-start.54
  388.8 17.7 %copy-start.22 = (bf16[1,1024,768]{2,1,0:T(8,128)(2,1)S(1)}, bf16[1,1024,768]{2,1,0:T(8,128)(2,1)}, u32[]{:S(2)}) copy-start(bf16[1,1024,768]{2,1,0:T(8,128)(2,1)} %param.43) | copy-start | bytes 4718596
  388.8 17.6 %copy-start.63 = (f32[768]{0:T(1024)S(1)}, f32[768]{0:T(1024)}, u32[]{:S(2)}) copy-start(f32[768]{0:T(1024)} %param.42) | copy-start | bytes 9220
  388.9 37.6 %all-gather.17.cloned.1.call-start = ((), (), s32[]{:S(2)}) async-start(), calls=%async_computation.12 | async-start | bytes 4718592 | tf_op jit(solution)/shard_map/all_gather | solution.py:171
  406.5 20.0 %copy-start.30 = (bf16[384,768]{0,1:T(8,128)(2,1)S(1)}, bf16[384,768]{0,1:T(8,128)(2,1)}, u32[]{:S(2)}) copy-start(bf16[384,768]{0,1:T(8,128)(2,1)} %all_gather.34) | copy-start | bytes 1769476
  413.0 414.2 %reduce-scatter.11.cloned.1.call-start = ((), (), s32[]{:S(2)}) async-start(), calls=%async_computation.13 | async-start | bytes 9437184 | tf_op jit(solution)/shard_map/reduce_scatter | solution.py:242
  435.4 4.4 copy-start.3
  435.4 4.4 copy-start.34
  781.9 4.5 copy-start.14
  783.6 4.6 copy-start.16
  783.7 2.8 copy-start.26
  786.4 3.8 copy-start.18
  794.7 434.6 %all-reduce.7.cloned.1.call-start = ((), (), s32[]{:S(2)}) async-start(), calls=%async_computation.15 | async-start | bytes 28311552 | tf_op jit(solution)/shard_map/psum | solution.py:297
  794.7 9.8 copy-start.66
  804.6 11.0 copy-start.13
  804.6 11.0 copy-start.67
  815.5 2.9 copy-start.17
  815.5 2.9 copy-start.65
  818.5 2.9 copy-start.15
  821.3 2.9 copy-start.19
  827.1 545.0 %all-reduce.5.cloned.1.call-start = ((), (), s32[]{:S(2)}) async-start(), calls=%async_computation.14 | async-start | bytes 6144000 | tf_op jit(solution)/shard_map/psum | solution.py:274
  828.5 3.6 copy-start.11
  1238.4 137.4 %copy-start.1 = (f32[1000,768]{1,0:T(8,128)S(1)}, f32[1000,768]{1,0:T(8,128)}, u32[]{:S(2)}) copy-start(f32[1000,768]{1,0:T(8,128)} %param.27) | copy-start | bytes 9216004
  (31 other events, 49.7 us)
Sparse Core Ops, SparseCore 0:
  14.7 14.8 all-gather.6
  240.1 14.7 reduce-scatter.4
  413.1 13.3 all-gather.16
  794.8 15.6 reduce-scatter.10
  827.2 402.0 all-reduce.6
  1236.1 135.9 all-reduce.4
Sparse Core Ops, SparseCore 1:
  242.9 37.5 all-gather.10
  282.5 12.0 all-gather.8
  296.0 13.2 all-gather.14
  311.9 38.5 all-gather.12
  377.8 14.3 reduce-scatter.8
  394.5 12.0 reduce-scatter.6
where the time goes:
time: 1390 us; the launch traced here: 1380 us
  waiting for transfers between devices  567 us (41%)
  matrix products  470 us (34%)
  other arithmetic  177 us (13%)
  blocking collectives  91.2 us (7%)
  local copies, waits for them, and re-layouts  60.1 us (4%)
  between operations  17.5 us (1%)
    psum x1, waiting for transfers between devices, shards(): lax.psum((grad_w_query, grad_w_key, grad_w_value, grad_up, grad_out_proj,...  342 us
    psum x1, waiting for transfers between devices, shards(): lax.psum((grad_table, grad_gain_one, grad_bias_one, wide_query_bias, wide...  131 us
    dot_general x8, matrix products, scores_for(): jnp.einsum('qhd,khd->hqk', query_part, key_part, preferred_element_type=j...  91.3 us
    convert_element_type x4, other arithmetic, backward_block(): grad_scores = (probs * (grad_probs - inner_sum)).astype(jnp.bfloat16)  85 us
    dot_general x4, matrix products, backward_block(): jnp.einsum('qhd,khd->hqk', grad_part, value_part, preferred_element_type=...  72.5 us
    dot_general x4, matrix products, backward_block(): jnp.einsum('hqk,qhd->khd', probs.astype(jnp.bfloat16), grad_part, preferr...  54.3 us
    reduce_sum x4, other arithmetic, forward_block(): total = jnp.sum(expo, axis=-1, keepdims=True)  48.3 us
    dot_general x4, matrix products, forward_block(): jnp.einsum('hqk,khd->qhd', probs, value_part, preferred_element_type=jnp....  46.5 us
  transfers between devices with their start and end apart: 12, of which 9 were waited for; matrix products, arithmetic and copies ran while one was open for 8% of the time, Pallas kernels for 0%

commit v1 on v0

--- a/solution.py
+++ b/solution.py
@@ -272,19 +272,22 @@
         sum_up_bias,
         sum_down_bias,
     ) = lax.psum(
-        (
-            grad_table,
-            grad_gain_one,
-            grad_bias_one,
-            wide_query_bias,
-            wide_value_bias,
-            grad_b_out,
-            grad_gain_two,
-            grad_bias_two,
-            wide_up_bias,
-            grad_b_down,
+        lax.psum(
+            (
+                grad_table,
+                grad_gain_one,
+                grad_bias_one,
+                wide_query_bias,
+                wide_value_bias,
+                grad_b_out,
+                grad_gain_two,
+                grad_bias_two,
+                wide_up_bias,
+                grad_b_down,
+            ),
+            ("row", "col"),
         ),
-        ("dp", "row", "col"),
+        "dp",
     )
     grad_b_query = lax.dynamic_slice_in_dim(sum_query_bias, col_index * head_cols, head_cols, 0)
     grad_b_value = lax.dynamic_slice_in_dim(sum_value_bias, col_index * head_cols, head_cols, 0)

time: 1390 us -> 1440 us (1.036)
  waiting for transfers between devices: 567 us -> 616 us
    psum x0 -> x1, waiting for transfers between devices: none -> 108 us  [shards(): lax.psum(lax.psum((grad_table, grad_gain_one, grad_bias_one, wide_query_b...]
    psum x1, waiting for transfers between devices: 131 us -> 56.4 us  [shards(): lax.psum((grad_table, grad_gain_one, grad_bias_one, wide_query_bias, wide...]
    psum x0 -> x1, blocking collectives: none -> 22.4 us  [shards(): lax.psum(lax.psum((grad_table, grad_gain_one, grad_bias_one, wide_query_b...]
    psum x1, blocking collectives: 46.3 us -> 24.9 us  [shards(): lax.psum((grad_table, grad_gain_one, grad_bias_one, wide_query_bias, wide...]
    psum x1, waiting for transfers between devices: 342 us -> 358 us  [shards(): lax.psum((grad_w_query, grad_w_key, grad_w_value, grad_up, grad_out_proj,...]
  transfers between devices with their start and end apart: 12 -> 13, of which waited for: 9 -> 10; matrix products, arithmetic and copies ran while one was open for 8% -> 7% of each run, Pallas kernels for 0% -> 0%
where the time goes in v1:
time: 1440 us; the launch traced here: 1430 us
  waiting for transfers between devices  616 us (43%)
  matrix products  471 us (33%)
  other arithmetic  176 us (12%)
  blocking collectives  92.3 us (6%)
  local copies, waits for them, and re-layouts  59 us (4%)
  between operations  17.6 us (1%)
    psum x1, waiting for transfers between devices, shards(): lax.psum((grad_w_query, grad_w_key, grad_w_value, grad_up, grad_out_proj,...  358 us
    psum x1, waiting for transfers between devices, shards(): lax.psum(lax.psum((grad_table, grad_gain_one, grad_bias_one, wide_query_b...  108 us
    dot_general x8, matrix products, scores_for(): jnp.einsum('qhd,khd->hqk', query_part, key_part, preferred_element_type=j...  90.5 us
    convert_element_type x4, other arithmetic, backward_block(): grad_scores = (probs * (grad_probs - inner_sum)).astype(jnp.bfloat16)  84.9 us
    dot_general x4, matrix products, backward_block(): jnp.einsum('qhd,khd->hqk', grad_part, value_part, preferred_element_type=...  72.5 us
    psum x1, waiting for transfers between devices, shards(): lax.psum((grad_table, grad_gain_one, grad_bias_one, wide_query_bias, wide...  56.4 us
    dot_general x4, matrix products, backward_block(): jnp.einsum('hqk,qhd->khd', probs.astype(jnp.bfloat16), grad_part, preferr...  53.9 us
    reduce_sum x4, other arithmetic, forward_block(): total = jnp.sum(expo, axis=-1, keepdims=True)  48.3 us
  transfers between devices with their start and end apart: 13, of which 10 were waited for; matrix products, arithmetic and copies ran while one was open for 7% of the time, Pallas kernels for 0%

profile of v1, /device:TPU:0, one launch (start us, length us, event | category | flops | bytes accessed | tf_op | source)
XLA Modules:
  0.0 1434.1 jit_solution(9562234132266401281)
XLA Ops:
  16.0 12.6 all_gather.34
  28.7 11.2 all_gather.33
  39.9 10.9 all_gather.32
  50.8 10.1 all_gather.31
  61.8 4.8 add_convert_fusion.4
  81.4 148.8 %while.47 = (s32[]{:T(128)}, bf16[4,512,6,64]{1,3,2,0:T(8,128)(2,1)}, f32[4,6,512]{2,1,0:T(8,128)}, s32[2048]{0:T(1024)S(1)}, s32[4,512]{1,0:T(4,128)S(1)}, /*in...) while((s32[]{:T(128)}, ...), condition=%wide.region_5.6_spmd, body=%wide.region_2.5_spmd.sunk | while | flops 1687155712 | bytes 103016640 | solution.py:123
  82.0 11.5 fusion.135
  93.6 12.1 fusion.136
  105.7 11.6 fusion.137
  119.1 11.5 fusion.135
  130.7 12.1 fusion.136
  142.8 11.6 fusion.137
  156.2 11.5 fusion.135
  167.8 12.1 fusion.136
  179.9 11.6 fusion.137
  193.3 11.5 fusion.135
  204.9 12.1 fusion.136
  217.0 11.6 fusion.137
  241.7 12.8 reduce-scatter.5.cloned.1.call-done
  262.0 18.1 %all-gather.11.cloned.1.call-done = bf16[768,1536]{1,0:T(8,128)(2,1)} async-done(((bf16[192,1536]{1,0:T(8,128)(2,1)}), bf16[768,1536]{1,0:T(8,128)(2,1)}) %all-gather.11.cloned.1.call-update) | async-done | bytes 2359312 | tf_op jit(solution)/shard_map/all_gather | solution.py:73
  280.0 14.1 all-gather.9.cloned.1.call-done
  294.1 34.8 %multiply_convert_fusion.1 = (bf16[2048,1536]{1,0:T(8,128)(2,1)}, f32[2048,1536]{1,0:T(8,128)}, f32[2048,1536]{1,0:T(8,128)}) fusion(f32[1536]{0:T(1024)S(1)} %copy-done.69, bf16[768,1536]{1,0:T(8,128)(2,1)} %all-gather.11.cloned.1.call-done, bf16[1,2048,768]{2,1,0:T(8,128)(2,1)} %all-gather.9.cloned.1.call-done), kind=kOutput, calls=%fused_computation.51 | convolution fusion | flops 5039456256 | bytes 36968448 | tf_op jit(solution)/shard_map/dot_general | solution.py:138
  329.0 21.0 %all-gather.13.cloned.1.call-done = bf16[1536,768]{0,1:T(8,128)(2,1)} async-done(((bf16[1536,192]{0,1:T(8,128)(2,1)}), bf16[1536,768]{0,1:T(8,128)(2,1)}) %all-gather.13.cloned.1.call-update) | async-done | bytes 2359312 | tf_op jit(solution)/shard_map/all_gather | solution.py:75
  350.0 17.7 %convert_reduce_fusion = (f32[1536]{0:T(1024)}, bf16[2048,1536]{1,0:T(8,128)(2,1)S(1)}) fusion(f32[2048,1536]{1,0:T(8,128)} %get-tuple-element.334, bf16[1536,768]{0,1:T(8,128)(2,1)} %all-gather.13.cloned.1.call-done, bf16[1,2048,768]{2,1,0:T(8,128)(2,1)} %all-gather.15.cloned.1.call-done, f32[2048,1536]{1,0:T(8,128)} %get-tuple-element.343, ...), kind=kOutput, calls=%fused_computation.49 | convolution fusion | flops 4885314048 | bytes 36974592 | tf_op jit(solution)/shard_map/rd,fd->rf/dot_general | solution.py:155
  370.3 7.0 convolution_bitcast_fusion
  378.9 9.4 fusion.67
  396.0 10.1 reduce-scatter.7.cloned.1.call-done
  406.1 6.4 convert_reduce_fusion.2
  412.6 13.5 all-gather.17.cloned.1.call-done
  426.1 4.9 fusion.75
  439.4 338.9 %while.48 = (s32[]{:T(128)}, f32[2048,6,64]{0,2,1:T(8,128)}, f32[2048,6,64]{0,2,1:T(8,128)}, bf16[4,512,6,64]{1,3,2,0:T(8,128)(2,1)}, bf16[4,512,6,64]{1,3,2,0:T...) while((s32[]{:T(128)}, f32[2048,6,64]{0,2,1:T(8,128)}, ...), condition=%wide.region_15.16_spmd.clone, body=%wide.region_13.15_spmd.clone.sunk | while | flops 4126077952 | bytes 212699312 | solution.py:216
  441.9 11.1 fusion.147
  453.0 12.8 bitcast_add_fusion.5
  465.8 18.1 %multiply_reduce_fusion.10 = (f32[6,512]{1,0:T(8,128)S(1)}, f32[6,512,2048]{2,1,0:T(8,128)}) fusion(f32[6,512,2048]{2,1,0:T(8,128)} %fusion.147, f32[6,512]{1,0:T(8,128)S(1)} %dynamic-slice_bitcast_fusion.2, pred[512,2048]{1,0:T(8,128)(4,1)S(1)} %broadcast_compare_fusion.5, bf16[2048,6,64]{0,2,1:T(8,128)(2,1)} %get-tuple-element.535, ...), kind=kOutput, calls=%fused_computation.18.clone.1 | convolution fusion | flops 836760576 | bytes 53370884 | tf_op jit(solution)/shard_map/while/body/eval_jaxpr/while/body/eval_jaxpr/qhd,khd->hqk/dot_general | solution.py:189
  483.9 21.2 %multiply_convert_fusion.3 = bf16[6,512,2048]{2,1,0:T(8,128)(2,1)} fusion(f32[6,512,2048]{2,1,0:T(8,128)} %get-tuple-element.470, f32[6,512,2048]{2,1,0:T(8,128)} %fusion.147, f32[6,512]{1,0:T(8,128)S(1)} %get-tuple-element.471, f32[6,512]{1,0:T(8,128)S(1)} %dynamic-slice_bitcast_fusion.2, pred[512,2048]{1,0:T(8,128)(4,1)S(1)} %broadcast_compare_fusion.5), kind=kLoop, calls=%fused_computation.17.clone.1 | loop fusion | flops 37748736 | bytes 63987712 | tf_op jit(solution)/shard_map/while/body/eval_jaxpr/while/body/eval_jaxpr/convert_element_type | solution.py:193
  505.1 9.3 fusion.148
  514.4 8.7 bitcast_add_fusion.4
  525.1 11.1 fusion.147
  536.2 13.7 bitcast_add_fusion.5
  549.9 18.1 %multiply_reduce_fusion.10 = (f32[6,512]{1,0:T(8,128)S(1)}, f32[6,512,2048]{2,1,0:T(8,128)}) fusion(f32[6,512,2048]{2,1,0:T(8,128)} %fusion.147, f32[6,512]{1,0:T(8,128)S(1)} %dynamic-slice_bitcast_fusion.2, pred[512,2048]{1,0:T(8,128)(4,1)S(1)} %broadcast_compare_fusion.5, bf16[2048,6,64]{0,2,1:T(8,128)(2,1)} %get-tuple-element.535, ...), kind=kOutput, calls=%fused_computation.18.clone.1 | convolution fusion | flops 836760576 | bytes 53370884 | tf_op jit(solution)/shard_map/while/body/eval_jaxpr/while/body/eval_jaxpr/qhd,khd->hqk/dot_general | solution.py:189
  568.0 21.2 %multiply_convert_fusion.3 = bf16[6,512,2048]{2,1,0:T(8,128)(2,1)} fusion(f32[6,512,2048]{2,1,0:T(8,128)} %get-tuple-element.470, f32[6,512,2048]{2,1,0:T(8,128)} %fusion.147, f32[6,512]{1,0:T(8,128)S(1)} %get-tuple-element.471, f32[6,512]{1,0:T(8,128)S(1)} %dynamic-slice_bitcast_fusion.2, pred[512,2048]{1,0:T(8,128)(4,1)S(1)} %broadcast_compare_fusion.5), kind=kLoop, calls=%fused_computation.17.clone.1 | loop fusion | flops 37748736 | bytes 63987712 | tf_op jit(solution)/shard_map/while/body/eval_jaxpr/while/body/eval_jaxpr/convert_element_type | solution.py:193
  589.2 9.3 fusion.148
  598.5 9.6 bitcast_add_fusion.4
  610.1 11.1 fusion.147
  621.2 13.7 bitcast_add_fusion.5
  634.9 18.1 %multiply_reduce_fusion.10 = (f32[6,512]{1,0:T(8,128)S(1)}, f32[6,512,2048]{2,1,0:T(8,128)}) fusion(f32[6,512,2048]{2,1,0:T(8,128)} %fusion.147, f32[6,512]{1,0:T(8,128)S(1)} %dynamic-slice_bitcast_fusion.2, pred[512,2048]{1,0:T(8,128)(4,1)S(1)} %broadcast_compare_fusion.5, bf16[2048,6,64]{0,2,1:T(8,128)(2,1)} %get-tuple-element.535, ...), kind=kOutput, calls=%fused_computation.18.clone.1 | convolution fusion | flops 836760576 | bytes 53370884 | tf_op jit(solution)/shard_map/while/body/eval_jaxpr/while/body/eval_jaxpr/qhd,khd->hqk/dot_general | solution.py:189
  653.0 21.2 %multiply_convert_fusion.3 = bf16[6,512,2048]{2,1,0:T(8,128)(2,1)} fusion(f32[6,512,2048]{2,1,0:T(8,128)} %get-tuple-element.470, f32[6,512,2048]{2,1,0:T(8,128)} %fusion.147, f32[6,512]{1,0:T(8,128)S(1)} %get-tuple-element.471, f32[6,512]{1,0:T(8,128)S(1)} %dynamic-slice_bitcast_fusion.2, pred[512,2048]{1,0:T(8,128)(4,1)S(1)} %broadcast_compare_fusion.5), kind=kLoop, calls=%fused_computation.17.clone.1 | loop fusion | flops 37748736 | bytes 63987712 | tf_op jit(solution)/shard_map/while/body/eval_jaxpr/while/body/eval_jaxpr/convert_element_type | solution.py:193
  674.3 9.3 fusion.148
  683.5 9.6 bitcast_add_fusion.4
  695.2 11.1 fusion.147
  706.3 13.7 bitcast_add_fusion.5
  720.0 18.1 %multiply_reduce_fusion.10 = (f32[6,512]{1,0:T(8,128)S(1)}, f32[6,512,2048]{2,1,0:T(8,128)}) fusion(f32[6,512,2048]{2,1,0:T(8,128)} %fusion.147, f32[6,512]{1,0:T(8,128)S(1)} %dynamic-slice_bitcast_fusion.2, pred[512,2048]{1,0:T(8,128)(4,1)S(1)} %broadcast_compare_fusion.5, bf16[2048,6,64]{0,2,1:T(8,128)(2,1)} %get-tuple-element.535, ...), kind=kOutput, calls=%fused_computation.18.clone.1 | convolution fusion | flops 836760576 | bytes 53370884 | tf_op jit(solution)/shard_map/while/body/eval_jaxpr/while/body/eval_jaxpr/qhd,khd->hqk/dot_general | solution.py:189
  738.1 21.2 %multiply_convert_fusion.3 = bf16[6,512,2048]{2,1,0:T(8,128)(2,1)} fusion(f32[6,512,2048]{2,1,0:T(8,128)} %get-tuple-element.470, f32[6,512,2048]{2,1,0:T(8,128)} %fusion.147, f32[6,512]{1,0:T(8,128)S(1)} %get-tuple-element.471, f32[6,512]{1,0:T(8,128)S(1)} %dynamic-slice_bitcast_fusion.2, pred[512,2048]{1,0:T(8,128)(4,1)S(1)} %broadcast_compare_fusion.5), kind=kLoop, calls=%fused_computation.17.clone.1 | loop fusion | flops 37748736 | bytes 63987712 | tf_op jit(solution)/shard_map/while/body/eval_jaxpr/while/body/eval_jaxpr/convert_element_type | solution.py:193
  759.3 9.3 fusion.148
  768.6 9.6 bitcast_add_fusion.4
  788.8 4.5 add_bitcast_fusion
  793.4 9.8 fusion.48
  803.3 10.9 fusion.45
  823.8 4.9 fusion.41
  837.4 56.4 %all-reduce.7.cloned.1.call-done = f32[1000,768]{1,0:T(8,128)} async-done(((f32[1000,768]{1,0:T(8,128)}), f32[1000,768]{1,0:T(8,128)}) %all-reduce.7.cloned.1.call-update) | async-done | bytes 3072016 | tf_op jit(solution)/shard_map/psum | solution.py:275
  895.0 24.9 %all-reduce.1 = (f32[768]{0:T(1024)S(1)}, f32[768]{0:T(1024)S(1)}, f32[768]{0:T(1024)S(1)}, f32[768]{0:T(1024)S(1)}, f32[768]{0:T(1024)S(1)}, /*index=5*/f32[768...) all-reduce(f32[768]{0:T(1024)S(1)} %get-tuple-element.258, ...), channel_id=1, replica_groups=mesh['dp'=4,'row'=4,'col'=2] {'row','col'}, use_global_device_ids=true, to_apply=%region_23.24 | all-reduce | flops 9216 | bytes 73728 | tf_op jit(solution)/shard_map/psum | solution.py:275
  920.0 22.4 %all-reduce.2 = (f32[768]{0:T(1024)}, f32[768]{0:T(1024)}, f32[768]{0:T(1024)S(1)}, f32[768]{0:T(1024)S(1)}, f32[768]{0:T(1024)}, /*index=5*/f32[768]{0:T(1024)}...) all-reduce(f32[768]{0:T(1024)S(1)} %get-tuple-element.308, ...), channel_id=1, replica_groups=mesh['dp'=4,'row'=4,'col'=2] {'dp'}, use_global_device_ids=true, to_apply=%region_24.25 | all-reduce | flops 9216 | bytes 73728 | tf_op jit(solution)/shard_map/psum | solution.py:274
  944.3 358.1 %all-reduce.11.cloned.1.call-done = (f32[768,384]{1,0:T(8,128)}, f32[768,384]{1,0:T(8,128)}, f32[768,384]{1,0:T(8,128)}, f32[384,768]{0,1:T(8,128)}, f32[768,1536]{1,0:T(8,128)}, /*index=5*/f32[1536,768]{0,1:T(8,128)}) async-done(((f32[768,384]{1,0:T(8,128)}, f32[768,384]{1,0:T(8,128)}, f32[768,384]{1,0:T(8,128)}, f32[384,768]{0,1:T(8,128)}, f32[768,1536]{1,0:T(8,128)}, /*index=5*/f32[1536,768]{0,1:T(8,128)}), ...) | async-done | bytes 14155792 | tf_op jit(solution)/shard_map/psum | solution.py:300
  1314.2 108.5 %all-reduce.9.cloned.1.call-done = f32[1000,768]{1,0:T(8,128)} async-done(((f32[1000,768]{1,0:T(8,128)}), f32[1000,768]{1,0:T(8,128)}) %all-reduce.9.cloned.1.call-update) | async-done | bytes 3072016 | tf_op jit(solution)/shard_map/psum | solution.py:274
  (292 shorter events, 124.4 us)
Async XLA Ops:
  8.0 4.7 copy-start.51
  8.1 4.7 copy-start.60
  8.1 52.9 %all-gather.7.cloned.1.call-start = ((), (), s32[]{:S(2)}) async-start(), calls=%async_computation.4 | async-start | bytes 4718592 | tf_op jit(solution)/shard_map/all_gather | solution.py:85
  8.1 3.4 copy-start.5
  12.0 3.9 copy-start.35
  12.0 4.0 copy-start.36
  14.6 47.2 %copy-start.70 = (f32[384]{0:T(512)S(1)}, f32[384]{0:T(512)}, u32[]{:S(2)}) copy-start(f32[384]{0:T(512)} %param.33) | copy-start | bytes 4612
  14.6 239.8 %reduce-scatter.5.cloned.1.call-start = ((), (), s32[]{:S(2)}) async-start(), calls=%async_computation.5 | async-start | bytes 9437184 | tf_op jit(solution)/shard_map/reduce_scatter | solution.py:132
  73.8 3.5 copy-start.23
  73.8 3.5 copy-start.64
  73.8 3.5 copy-start.71
  93.6 12.1 copy-start.8
  93.6 12.1 copy-start.20
  130.7 12.1 copy-start.8
  130.7 12.1 copy-start.20
  167.8 12.1 copy-start.8
  167.8 12.1 copy-start.20
  204.9 12.1 copy-start.8
  204.9 12.1 copy-start.20
  230.1 3.7 copy-start.2
  230.2 3.7 copy-start.46
  230.2 4.8 copy-start.29
  239.5 15.0 %copy-start.6 = (bf16[1,1024,768]{2,1,0:T(8,128)(2,1)S(1)}, bf16[1,1024,768]{2,1,0:T(8,128)(2,1)}, u32[]{:S(2)}) copy-start(bf16[1,1024,768]{2,1,0:T(8,128)(2,1)} %param.24) | copy-start | bytes 4718596
  239.5 15.0 %copy-start.40 = (f32[768]{0:T(1024)S(1)}, f32[768]{0:T(1024)}, u32[]{:S(2)}) copy-start(f32[768]{0:T(1024)} %copy-done.39) | copy-start | bytes 9220
  239.5 15.0 %copy-start.61 = (f32[768]{0:T(1024)S(1)}, f32[768]{0:T(1024)}, u32[]{:S(2)}) copy-start(f32[768]{0:T(1024)} %param.36) | copy-start | bytes 9220
  239.5 40.5 %all-gather.11.cloned.1.call-start = ((), (), s32[]{:S(2)}) async-start(), calls=%async_computation.7 | async-start | bytes 2949120 | tf_op jit(solution)/shard_map/all_gather | solution.py:73
  241.7 52.5 %all-gather.9.cloned.1.call-start = ((), (), s32[]{:S(2)}) async-start(), calls=%async_computation.6 | async-start | bytes 4718592 | tf_op jit(solution)/shard_map/all_gather | solution.py:135
  260.3 33.8 %copy-start.69 = (f32[1536]{0:T(1024)S(1)}, f32[1536]{0:T(1024)}, u32[]{:S(2)}) copy-start(f32[1536]{0:T(1024)} %param.40) | copy-start | bytes 18436
  260.4 68.6 %all-gather.15.cloned.1.call-start = ((), (), s32[]{:S(2)}) async-start(), calls=%async_computation.10 | async-start | bytes 4718592 | tf_op jit(solution)/shard_map/all_gather | solution.py:148
  261.0 89.0 %all-gather.13.cloned.1.call-start = ((), (), s32[]{:S(2)}) async-start(), calls=%async_computation.8 | async-start | bytes 2949120 | tf_op jit(solution)/shard_map/all_gather | solution.py:75
  261.9 129.9 %reduce-scatter.9.cloned.1.call-start = ((), (), s32[]{:S(2)}) async-start(), calls=%async_computation.11 | async-start | bytes 9437184 | tf_op jit(solution)/shard_map/reduce_scatter | solution.py:165
  350.0 20.3 %copy-start.67 = (bf16[768,1536]{1,0:T(8,128)(2,1)S(1)}, bf16[768,1536]{1,0:T(8,128)(2,1)}, u32[]{:S(2)}) copy-start(bf16[768,1536]{1,0:T(8,128)(2,1)} %all-gather.11.cloned.1.call-done) | copy-start | bytes 7077892
  377.3 28.7 %reduce-scatter.7.cloned.1.call-start = ((), (), s32[]{:S(2)}) async-start(), calls=%async_computation.9 | async-start | bytes 4718592 | tf_op jit(solution)/shard_map/reduce_scatter | solution.py:143
  388.4 3.4 copy-start.45
  388.4 3.4 copy-start.50
  388.4 3.4 copy-start.54
  388.4 17.6 %copy-start.22 = (bf16[1,1024,768]{2,1,0:T(8,128)(2,1)S(1)}, bf16[1,1024,768]{2,1,0:T(8,128)(2,1)}, u32[]{:S(2)}) copy-start(bf16[1,1024,768]{2,1,0:T(8,128)(2,1)} %param.43) | copy-start | bytes 4718596
  388.4 17.6 %copy-start.63 = (f32[768]{0:T(1024)S(1)}, f32[768]{0:T(1024)}, u32[]{:S(2)}) copy-start(f32[768]{0:T(1024)} %param.42) | copy-start | bytes 9220
  388.4 37.6 %all-gather.17.cloned.1.call-start = ((), (), s32[]{:S(2)}) async-start(), calls=%async_computation.12 | async-start | bytes 4718592 | tf_op jit(solution)/shard_map/all_gather | solution.py:171
  406.0 20.0 %copy-start.30 = (bf16[384,768]{0,1:T(8,128)(2,1)S(1)}, bf16[384,768]{0,1:T(8,128)(2,1)}, u32[]{:S(2)}) copy-start(bf16[384,768]{0,1:T(8,128)(2,1)} %all_gather.34) | copy-start | bytes 1769476
  412.5 401.7 %reduce-scatter.11.cloned.1.call-start = ((), (), s32[]{:S(2)}) async-start(), calls=%async_computation.13 | async-start | bytes 9437184 | tf_op jit(solution)/shard_map/reduce_scatter | solution.py:242
  435.0 4.4 copy-start.3
  435.0 4.4 copy-start.34
  780.6 4.5 copy-start.14
  782.3 4.6 copy-start.16
  785.1 3.7 copy-start.18
  793.4 100.4 %all-reduce.7.cloned.1.call-start = ((), (), s32[]{:S(2)}) async-start(), calls=%async_computation.14 | async-start | bytes 6144000 | tf_op jit(solution)/shard_map/psum | solution.py:275
  793.4 9.8 copy-start.66
  803.3 11.0 copy-start.7
  803.3 11.0 copy-start.41
  803.3 11.0 copy-start.43
  803.3 11.0 copy-start.48
  803.3 11.0 copy-start.52
  823.5 479.0 %all-reduce.11.cloned.1.call-start = ((), (), s32[]{:S(2)}) async-start(), calls=%async_computation.16 | async-start | bytes 28311552 | tf_op jit(solution)/shard_map/psum | solution.py:300
  823.8 4.9 copy-start.17
  823.8 4.9 copy-start.65
  837.3 56.6 %copy-start.59 = (f32[1536]{0:T(1024)S(1)}, f32[1536]{0:T(1024)}, u32[]{:S(2)}) copy-start(f32[1536]{0:T(1024)} %get-tuple-element.344) | copy-start | bytes 18436
  837.3 56.9 %copy-start.10 = (bf16[4,512,6,64]{1,3,2,0:T(8,128)(2,1)S(1)}, bf16[4,512,6,64]{1,3,2,0:T(8,128)(2,1)}, u32[]{:S(2)}) copy-start(bf16[4,512,6,64]{1,3,2,0:T(8,128)(2,1)} %get-tuple-element.179) | copy-start | bytes 4718596
  837.3 57.7 %copy-start.55 = (f32[768]{0:T(1024)S(1)}, f32[768]{0:T(1024)}, u32[]{:S(2)}) copy-start(f32[768]{0:T(1024)} %get-tuple-element.256) | copy-start | bytes 9220
  837.3 57.7 %copy-start.56 = (f32[768]{0:T(1024)S(1)}, f32[768]{0:T(1024)}, u32[]{:S(2)}) copy-start(f32[768]{0:T(1024)} %get-tuple-element.262) | copy-start | bytes 9220
  837.3 57.7 %copy-start.57 = (f32[768]{0:T(1024)S(1)}, f32[768]{0:T(1024)}, u32[]{:S(2)}) copy-start(f32[768]{0:T(1024)} %get-tuple-element.326) | copy-start | bytes 9220
  837.3 57.7 %copy-start.58 = (f32[768]{0:T(1024)S(1)}, f32[768]{0:T(1024)}, u32[]{:S(2)}) copy-start(f32[768]{0:T(1024)} %get-tuple-element.342) | copy-start | bytes 9220
  837.4 585.4 %all-reduce.9.cloned.1.call-start = ((), (), s32[]{:S(2)}) async-start(), calls=%async_computation.15 | async-start | bytes 6144000 | tf_op jit(solution)/shard_map/psum | solution.py:274
  1311.7 114.7 %copy-start.1 = (f32[1000,768]{1,0:T(8,128)S(1)}, f32[1000,768]{1,0:T(8,128)}, u32[]{:S(2)}) copy-start(f32[1000,768]{1,0:T(8,128)} %param.27) | copy-start | bytes 9216004
  (31 other events, 66.9 us)
Sparse Core Ops, SparseCore 0:
  14.7 14.8 all-gather.6
  239.6 14.7 reduce-scatter.4
  412.6 13.3 all-gather.16
  793.5 15.6 reduce-scatter.10
  823.6 70.1 all-reduce.6
  901.2 401.2 all-reduce.10
  1305.0 117.6 all-reduce.8
Sparse Core Ops, SparseCore 1:
  242.4 37.6 all-gather.10
  282.1 12.0 all-gather.8
  295.6 13.2 all-gather.14
  311.4 38.5 all-gather.12
  377.4 14.3 reduce-scatter.8
  394.0 11.9 reduce-scatter.6
